TPU v7x, 32 devices: a whole 2x2x4 slice. The times are simulated.
32 devices in a mesh: section: 4 (over x, core), expert: 8 (over z, y).
Axes of the slice: x: 2, y: 2, z: 4, core: 2. Of those that a mesh axis runs over, the one named last changes fastest.
Arguments:
- tokens: bfloat16 [4, 512, 4096], P('section', 'expert'), may hold values from -6 to 6
- out_grad: bfloat16 [4, 512, 4096], P('section', 'expert'), may hold values from -6 to 6
- expert_ids: int32 [4, 512, 2], P('section', 'expert'), may hold values from 0 to 7, as said below
- slot_ids: int32 [4, 512, 2], P('section', 'expert'), may hold values from 0 to 15, as said below
- gate_int: int32 [4, 512, 2], P('section', 'expert'), may hold values from 16 to 255
- saved_gate: bfloat16 [4, 128, 14336], P('section', None, 'expert'), may hold values from -6 to 6
- saved_up: bfloat16 [4, 128, 14336], P('section', None, 'expert'), may hold values from -6 to 6
- w_gate: bfloat16 [4, 4096, 14336], P('section', None, 'expert'), may hold values from -0.09375 to 0.09375
- w_up: bfloat16 [4, 4096, 14336], P('section', None, 'expert'), may hold values from -0.09375 to 0.09375
- w_down: bfloat16 [4, 14336, 4096], P('section', 'expert'), may hold values from -0.0625 to 0.0625
Outputs:
- arriving_grad: bfloat16 [4, 512, 4096], P('section', 'expert')
- grad_w_gate: bfloat16 [4, 4096, 14336], P('section', None, 'expert')
- grad_w_up: bfloat16 [4, 4096, 14336], P('section', None, 'expert')
- grad_w_down: bfloat16 [4, 14336, 4096], P('section', 'expert')
Inputs may be any that keep to these rules, and one draw needn't show every extreme that they name: `expert_ids`: in each section, the 64 tokens of each index of expert name each of the 8 experts exactly 16 times; a token's two experts differ. `slot_ids`: for each expert, the slots of the 64 tokens of one index of expert that name it are 0 to 15, each once.
All inputs are finite; a program needn't handle non-finite values.
Results may differ from a plain program's by a relative error of at most 0.018.
Values may be sent and summed in bfloat16 or wider, within the bound.
No kernel may reach another device: no remote copies, remote signals or barrier semaphores. Data moves between devices by JAX's collectives and lax.ppermute only.
A program may use at most 128 MiB of HBM per device.

v0:
```python
import functools

import jax
import jax.numpy as jnp
from jax import lax
from jax.experimental import pallas as pl
from jax.experimental.pallas import tpu as pltpu
from jax.sharding import PartitionSpec as P


EXPERTS = 8
E_WIN = 2
BF16 = jnp.bfloat16
F32 = jnp.float32
NT = (((1,), (1,)), ((), ()))
TN = (((0,), (0,)), ((), ()))
NN = (((1,), (0,)), ((), ()))
MIB = 2**20


def vmem():
    return pl.BlockSpec(memory_space=pltpu.VMEM)


def anywhere():
    return pl.BlockSpec(memory_space=pl.ANY)


def hbm():
    return pl.BlockSpec(memory_space=pltpu.HBM)


def smem():
    return pl.BlockSpec(memory_space=pltpu.SMEM)


def piece(total, wanted):
    for size in (wanted, 512, 256, 128):
        if size <= wanted and total % size == 0:
            return size
    return total


def like(shape, dtype=BF16):
    return jax.ShapeDtypeStruct(shape, dtype)


def params(mib):
    return pltpu.CompilerParams(vmem_limit_bytes=int(mib * MIB))


def placement(half, ids, slots, weights, capacity):
    rows = lax.broadcasted_iota(jnp.int32, (2 * capacity, ids.shape[1]), 0)
    matrix = jnp.zeros(rows.shape, F32)
    for k in range(2):
        expert = ids[k : k + 1, :]
        place = jnp.where(expert == half, 0, capacity) + slots[k : k + 1, :]
        hit = jnp.logical_and(rows == place, expert < E_WIN)
        matrix += jnp.where(hit, weights[k : k + 1, :], 0.0)
    return matrix.astype(BF16)


def pick_kernel(capacity, half_ref, *refs):
    sources, outs, copies, sems = refs[:5], refs[5:10], refs[10:15], refs[15]
    half = half_ref[0]
    flying = [
        pltpu.make_async_copy(source, copy, sems.at[n])
        for n, (source, copy) in enumerate(zip(sources, copies))
    ]
    for copy in flying:
        copy.start()
    for copy in flying[:4]:
        copy.wait()
    ids, slots, gates = (copies[n][...] for n in range(3))
    grads_own, grads_far, in_own, in_far, picks = outs
    scaled = placement(half, ids, slots, gates.astype(F32) / 256.0, capacity)
    plain = placement(half, ids, slots, jnp.ones(ids.shape, F32), capacity)
    rows = lax.dot_general(scaled, copies[3][...], NN, preferred_element_type=F32).astype(BF16)
    grads_own[...] = rows[:capacity]
    grads_far[...] = rows[capacity:]
    picks[...] = jnp.concatenate([plain[:capacity], plain[capacity:]], axis=1)
    flying[4].wait()
    rows = lax.dot_general(plain, copies[4][...], NN, preferred_element_type=F32).astype(BF16)
    in_own[...] = rows[:capacity]
    in_far[...] = rows[capacity:]


def pick(half, ids, slots, gates, grads, tokens, capacity):
    width = tokens.shape[1]
    sources = (ids, slots, gates, grads, tokens)
    return pl.pallas_call(
        functools.partial(pick_kernel, capacity),
        in_specs=[smem()] + [hbm()] * len(sources),
        out_specs=[vmem()] * 5,
        out_shape=[like((capacity, width))] * 4 + [like((capacity, 2 * ids.shape[1]))],
        scratch_shapes=[pltpu.VMEM(x.shape, x.dtype) for x in sources]
        + [pltpu.SemaphoreType.DMA((len(sources),))],
        compiler_params=params(8),
        cost_estimate=pl.CostEstimate(
            flops=2**36, bytes_accessed=6 * tokens.size, transcendentals=0
        ),
    )(half, *sources)


def saved_kernel(gate_hbm, up_hbm, hidden, act_ref, slope_ref, gate, up, sems):
    copies = [
        pltpu.make_async_copy(gate_hbm, gate, sems.at[0]),
        pltpu.make_async_copy(up_hbm, up, sems.at[1]),
    ]
    for copy in copies:
        copy.start()
    for copy in copies:
        copy.wait()
    g = gate[...].astype(F32)
    u = up[...].astype(F32)
    s = jax.nn.sigmoid(g)
    act = g * s
    hidden[...] = (act * u).astype(BF16)
    act_ref[...] = act
    slope_ref[...] = u * s * (1.0 + g * (1.0 - s))


def saved_stage(gate, up):
    shape = gate.shape
    return pl.pallas_call(
        saved_kernel,
        in_specs=[hbm()] * 2,
        out_specs=[vmem()] * 3,
        out_shape=[like(shape), like(shape, F32), like(shape, F32)],
        scratch_shapes=[pltpu.VMEM(shape, BF16)] * 2 + [pltpu.SemaphoreType.DMA((2,))],
        compiler_params=params(4),
        cost_estimate=pl.CostEstimate(
            flops=16 * gate.size, bytes_accessed=14 * gate.size, transcendentals=gate.size
        ),
    )(gate, up)


def hidden_kernel(capacity, pairs, index_ref, *refs):
    blocks = refs[: len(pairs)]
    act, slope, w_down, rows, gate_grad, up_grad, block_sems = refs[len(pairs) :]
    landings = land(capacity, pairs, index_ref[0], blocks, rows, block_sems)
    for copy in landings:
        copy.start()
    for copy in landings:
        copy.wait()
    units, step = w_down.shape[0], 256
    for start in range(0, units, step):
        some = slice(start, min(start + step, units))
        grad = lax.dot_general(w_down[some, :], rows[...], NT, preferred_element_type=F32).T
        gate_grad[:, some] = (grad * slope[:, some]).astype(BF16)
        up_grad[:, some] = (grad * act[:, some]).astype(BF16)


def hidden_stage(index, blocks, pairs, act, slope, w_down, capacity):
    units, width = w_down.shape
    total = act.shape[0]
    return pl.pallas_call(
        functools.partial(hidden_kernel, capacity, pairs),
        in_specs=[smem()] + [anywhere()] * len(blocks) + [vmem()] * 3,
        out_specs=[vmem()] * 3,
        out_shape=[like((total, width))] + [like((total, units))] * 2,
        scratch_shapes=[pltpu.SemaphoreType.DMA((total // capacity,))],
        compiler_params=params(6),
        cost_estimate=pl.CostEstimate(
            flops=2 * total * units * width, bytes_accessed=2 * units * width, transcendentals=0
        ),
    )(index, *blocks, act, slope, w_down)


def part_kernel(capacity, group, step, index_ref, *refs):
    gate_grad, up_grad, w_gate, up_hbm = refs[:4]
    outs = refs[4 : 4 + group]
    half, stage, w_up, sems = refs[4 + group :]
    index = index_ref[0]
    cuts = sems.shape[0]
    width = w_gate.shape[0]
    size = width // cuts
    ahead = [
        pltpu.make_async_copy(
            up_hbm.at[pl.ds(n * size, size)], w_up.at[pl.ds(n * size, size)], sems.at[n]
        )
        for n in range(cuts)
    ]
    for copy in ahead:
        copy.start()
    for start in range(0, width, step):
        some = slice(start, start + step)
        half[some, :] = lax.dot_general(
            w_gate[some, :], gate_grad[...], NT, preferred_element_type=F32
        )
    for n in range(cuts):
        ahead[n].wait()
        for start in range(n * size, (n + 1) * size, min(step, size)):
            some = slice(start, start + min(step, size))
            part = half[some, :] + lax.dot_general(
                w_up[some, :], up_grad[...], NT, preferred_element_type=F32
            )
            stage[:, some] = part.T.astype(BF16)
    for m in range(2 * group):
        source = pl.multiple_of(jnp.bitwise_xor(index, m) * capacity, capacity)
        start = m // group * capacity
        outs[m % group][start : start + capacity, :] = stage[pl.ds(source, capacity), :]


def part_stage(index, gate_grad, up_grad, w_gate, w_up, capacity, group):
    width, units = w_gate.shape
    total = gate_grad.shape[0]
    step = piece(width, 512)
    return pl.pallas_call(
        functools.partial(part_kernel, capacity, group, step),
        in_specs=[smem()] + [vmem()] * 3 + [hbm()],
        out_specs=[vmem()] * group,
        out_shape=[like((2 * capacity, width))] * group,
        scratch_shapes=[
            pltpu.VMEM((width, total), F32),
            pltpu.VMEM((total, width), BF16),
            pltpu.VMEM((width, units), BF16),
            pltpu.SemaphoreType.DMA((4,)),
        ],
        compiler_params=params(24),
        cost_estimate=pl.CostEstimate(
            flops=4 * total * units * width, bytes_accessed=4 * units * width, transcendentals=0
        ),
    )(index, gate_grad, up_grad, w_gate, w_up)


def land(capacity, pairs, index, blocks, rows, sems):
    copies = []
    for block, members in zip(blocks, pairs):
        for part, m in enumerate(members):
            start = pl.multiple_of(jnp.bitwise_xor(index, m) * capacity, capacity)
            copies.append(
                pltpu.make_async_copy(
                    block.at[pl.ds(part * capacity, capacity)],
                    rows.at[pl.ds(start, capacity)],
                    sems.at[m],
                )
            )
    return copies


def write_out(left, right, out, stage, sems):
    step = out.shape[0] // sems.shape[0]
    copies = []
    for n in range(sems.shape[0]):
        some = slice(n * step, (n + 1) * step)
        stage[some, :] = lax.dot_general(
            left[:, some], right[...], TN, preferred_element_type=F32
        ).astype(BF16)
        copy = pltpu.make_async_copy(
            stage.at[pl.ds(n * step, step)], out.at[pl.ds(n * step, step)], sems.at[n]
        )
        copy.start()
        copies.append(copy)
    return copies


def first_kernel(capacity, pairs, index_ref, *refs):
    blocks = refs[: len(pairs)]
    hidden, rows_grad, gate_grad, down, gate, rows_in = refs[len(pairs) : len(pairs) + 6]
    stage_down, stage_gate, sems_down, sems_gate, block_sems = refs[len(pairs) + 6 :]
    copies = land(capacity, pairs, index_ref[0], blocks, rows_in, block_sems)
    for copy in copies:
        copy.start()
    left = write_out(hidden, rows_grad, down, stage_down, sems_down)
    for copy in copies:
        copy.wait()
    left += write_out(rows_in, gate_grad, gate, stage_gate, sems_gate)
    for copy in left:
        copy.wait()


def weight_cost(count, total, units, width):
    return pl.CostEstimate(
        flops=2 * count * total * units * width,
        bytes_accessed=2 * count * units * width,
        transcendentals=0,
    )


def first_stage(index, blocks, pairs, hidden, rows_grad, gate_grad, capacity):
    total, units = hidden.shape
    width = rows_grad.shape[1]
    return pl.pallas_call(
        functools.partial(first_kernel, capacity, pairs),
        in_specs=[smem()] + [anywhere()] * len(blocks) + [vmem()] * 3,
        out_specs=[hbm(), hbm(), vmem()],
        out_shape=[like((units, width)), like((width, units)), like((total, width))],
        scratch_shapes=[
            pltpu.VMEM((units, width), BF16),
            pltpu.VMEM((width, units), BF16),
            pltpu.SemaphoreType.DMA((units // piece(units, 256),)),
            pltpu.SemaphoreType.DMA((width // piece(width, 512),)),
            pltpu.SemaphoreType.DMA((total // capacity,)),
        ],
        compiler_params=params(36),
        cost_estimate=weight_cost(2, total, units, width),
    )(index, *blocks, hidden, rows_grad, gate_grad)


def second_kernel(left, right, out, stage, sems):
    for copy in write_out(left, right, out, stage, sems):
        copy.wait()


def second_stage(rows_in, up_grad):
    total, width = rows_in.shape
    units = up_grad.shape[1]
    return pl.pallas_call(
        second_kernel,
        in_specs=[vmem()] * 2,
        out_specs=hbm(),
        out_shape=like((width, units)),
        scratch_shapes=[
            pltpu.VMEM((width, units), BF16),
            pltpu.SemaphoreType.DMA((width // piece(width, 256),)),
        ],
        compiler_params=params(24),
        cost_estimate=weight_cost(1, total, units, width),
    )(rows_in, up_grad)


def join_kernel(kept_ref, sent_ref, out_ref):
    tokens, width = out_ref.shape
    picks = kept_ref[:, width:]
    total = lax.dot_general(
        picks[:, :tokens], kept_ref[:, :width], TN, preferred_element_type=F32
    )
    total += lax.dot_general(
        picks[:, tokens : 2 * tokens], sent_ref[...], TN, preferred_element_type=F32
    )
    out_ref[...] = total.astype(BF16)


def join(kept, sent, tokens):
    return pl.pallas_call(
        join_kernel,
        in_specs=[vmem()] * 2,
        out_specs=vmem(),
        out_shape=like((tokens, sent.shape[1])),
        compiler_params=params(8),
    )(kept, sent)


def to_partner(value, m):
    peers = lax.axis_size("expert")
    return lax.ppermute(value, "expert", [(i, i ^ m) for i in range(peers)])


def to_behind(value, m):
    peers, layers = lax.axis_size("expert"), lax.axis_size("section")
    pairs = [
        (s * peers + i, (s - 1) * peers + (i ^ m)) for s in range(1, layers) for i in range(peers)
    ]
    return lax.ppermute(value, ("section", "expert"), pairs)


def shards(
    tokens, out_grad, expert_ids, slot_ids, gate_int, saved_gate, saved_up, w_gate, w_up, w_down
):
    peers = lax.axis_size("expert")
    group = peers // E_WIN
    capacity = tokens.shape[1] * 2 // EXPERTS
    stay = functools.partial(pltpu.with_memory_space_constraint, memory_space=pltpu.HBM)
    place = lax.axis_index("expert").astype(jnp.int32)
    index = place.reshape(1)
    half = (place // group).reshape(1)

    grads_own, grads_far, in_own, in_far, picks = pick(
        half,
        stay(expert_ids[0].T),
        stay(slot_ids[0].T),
        stay(gate_int[0].T),
        stay(out_grad[0]),
        stay(tokens[0]),
        capacity,
    )
    crossed = to_partner(grads_far, group)
    near = [grads_own] + [to_partner(grads_own, m) for m in range(1, group)]
    far = [crossed] + [to_partner(crossed, m) for m in range(1, group)]
    in_crossed = to_partner(in_far, group)
    hidden, act, slope = saved_stage(stay(saved_gate[0]), stay(saved_up[0]))
    singles = [(m,) for m in range(2 * group)]
    rows_grad, gate_grad, up_grad = hidden_stage(
        index,
        near + far,
        singles,
        act,
        slope,
        w_down[0],
        capacity,
    )
    both = jnp.concatenate([in_own, in_crossed], axis=0)
    in_blocks = [both] + [to_partner(both, m) for m in range(1, group)]
    parts = part_stage(
        index, gate_grad, up_grad, w_gate[0], stay(w_up[0]), capacity, group
    )
    returned = [to_partner(parts[m], m) for m in range(1, group)]
    pairs = [(m, m + group) for m in range(group)]
    grad_down, grad_gate, rows_in = first_stage(
        index, in_blocks, pairs, hidden, rows_grad, gate_grad, capacity
    )
    summed = parts[0].astype(F32)
    for part in returned:
        summed += part.astype(F32)
    summed = summed.astype(BF16)
    kept = jnp.concatenate([summed[:capacity], picks], axis=1)
    sent = summed[capacity:]
    sent = to_behind(sent, group)
    kept = to_behind(kept, 0)
    grad_up = second_stage(rows_in, up_grad)
    arriving = join(kept, sent, tokens.shape[1])
    return (arriving[None], grad_gate[None], grad_up[None], grad_down[None])


def solution(mesh):
    rows = P("section", "expert", None)
    columns = P("section", None, "expert")
    return jax.shard_map(
        shards,
        mesh=mesh,
        in_specs=(rows,) * 5 + (columns,) * 4 + (rows,),
        out_specs=(rows, columns, columns, rows),
        check_vma=False,
    )
```

profile of v0, /device:TPU:1, one launch (start us, length us, event | category | flops | bytes accessed | tf_op | source)
XLA Modules:
  0.0 75.5 jit_solution(8416086252397063434)
XLA Ops:
  0.6 0.0 slice-start
  0.7 0.0 copy-start
  0.7 0.0 slice-start.1
  0.7 0.0 slice-start.2
  0.7 0.0 slice-start.3
  0.7 1.7 %shard_map.129 = (bf16[16,4096]{1,0:T(8,128)(2,1)S(1)}, bf16[16,4096]{1,0:T(8,128)(2,1)S(1)}, bf16[16,4096]{1,0:T(8,128)(2,1)S(1)}, bf16[16,4096]{1,0:T(8,128)(2,1)S(1)}, bf16[16,128]{1,0:T(8,128)(2,1)S(1)}) custom-call(s32[1]{0:T(128)} %bitcast.1.half_ref, s32[2,64]{1,0:T(2,128)} %bitcast.33, s32[2,64]{1,0:T(2,128)} %bitcast.34, s32[2,64]{1,0:T(2,128)} %bitcast.35, ...), custom_call_target="tpu_custom_call" | custom-call | flops 68719476736 | bytes 1572864 | tf_op jit(solution)/shard_map/pallas_call | solution.py:91
  2.5 2.1 %collective-permute-start = (bf16[16,4096]{1,0:T(8,128)(2,1)S(1)}, bf16[16,4096]{1,0:T(8,128)(2,1)S(1)}, u32[]{:S(2)}, u32[]{:S(2)}) collective-permute-start(bf16[16,4096]{1,0:T(8,128)(2,1)S(1)} %get-tuple-element.22.refs_0_), channel_id=1, source_target_pairs={{0,1},{1,0},{2,3},{3,2},{4,5},{5,4},{6,7},{7,6},{8,9},{9,8},{10,11... | collective-permute-start | bytes 393224 | tf_op jit(solution)/shard_map/ppermute | solution.py:347
  4.6 1.3 %collective-permute-start.1 = (bf16[16,4096]{1,0:T(8,128)(2,1)S(1)}, bf16[16,4096]{1,0:T(8,128)(2,1)S(1)}, u32[]{:S(2)}, u32[]{:S(2)}) collective-permute-start(bf16[16,4096]{1,0:T(8,128)(2,1)S(1)} %get-tuple-element.22.refs_0_), channel_id=1, source_target_pairs={{0,2},{1,3},{2,0},{3,1},{4,6},{5,7},{6,4},{7,5},{8,10},{9,11},{10,... | collective-permute-start | bytes 393224 | tf_op jit(solution)/shard_map/ppermute | solution.py:347
  5.9 0.0 collective-permute-start.2
  5.9 2.4 %collective-permute-start.3 = (bf16[16,4096]{1,0:T(8,128)(2,1)S(1)}, bf16[16,4096]{1,0:T(8,128)(2,1)S(1)}, u32[]{:S(2)}, u32[]{:S(2)}) collective-permute-start(bf16[16,4096]{1,0:T(8,128)(2,1)S(1)} %get-tuple-element.23), channel_id=1, source_target_pairs={{0,4},{1,5},{2,6},{3,7},{4,0},{5,1},{6,2},{7,3},{8,12},{9,13},{10,... | collective-permute-start | bytes 393224 | tf_op jit(solution)/shard_map/ppermute | solution.py:347
  8.3 0.0 collective-permute-start.12
  8.3 2.5 %shard_map.130 = (bf16[128,1792]{1,0:T(8,128)(2,1)S(1)}, f32[128,1792]{1,0:T(8,128)S(1)}, f32[128,1792]{1,0:T(8,128)S(1)}) custom-call(bf16[128,1792]{1,0:T(8,128)(2,1)} %bitcast.29, bf16[128,1792]{1,0:T(8,128)(2,1)} %bitcast.30), custom_call_target="tpu_custom_call" | custom-call | flops 3670016 | bytes 3211264 | tf_op jit(solution)/shard_map/pallas_call | solution.py:125
  10.8 2.6 %collective-permute-done.3.refs_4_ = bf16[16,4096]{1,0:T(8,128)(2,1)S(1)} collective-permute-done((bf16[16,4096]{1,0:T(8,128)(2,1)S(1)}, bf16[16,4096]{1,0:T(8,128)(2,1)S(1)}, u32[]{:S(2)}, u32[]{:S(2)}) %collective-permute-start.3) | collective-permute-done | bytes 131104 | tf_op jit(solution)/shard_map/ppermute | solution.py:347
  13.4 0.2 collective-permute-start.4
  13.6 0.0 collective-permute-done.refs_1_
  13.6 3.5 %collective-permute-start.5 = (bf16[16,4096]{1,0:T(8,128)(2,1)S(1)}, bf16[16,4096]{1,0:T(8,128)(2,1)S(1)}, u32[]{:S(2)}, u32[]{:S(2)}) collective-permute-start(bf16[16,4096]{1,0:T(8,128)(2,1)S(1)} %collective-permute-done.3.refs_4_), channel_id=1, source_target_pairs={{0,2},{1,3},{2,0},{3,1},{4,6},{5,7},{6,4},{7,5},{8,10},{9,11},{10,... | collective-permute-start | bytes 393224 | tf_op jit(solution)/shard_map/ppermute | solution.py:347
  17.1 0.0 collective-permute-done.12
  17.1 3.8 %collective-permute-start.6 = (bf16[16,4096]{1,0:T(8,128)(2,1)S(1)}, bf16[16,4096]{1,0:T(8,128)(2,1)S(1)}, u32[]{:S(2)}, u32[]{:S(2)}) collective-permute-start(bf16[16,4096]{1,0:T(8,128)(2,1)S(1)} %collective-permute-done.3.refs_4_), channel_id=1, source_target_pairs={{0,3},{1,2},{2,1},{3,0},{4,7},{5,6},{6,5},{7,4},{8,11},{9,10},{10,... | collective-permute-start | bytes 393224 | tf_op jit(solution)/shard_map/ppermute | solution.py:347
  21.0 0.0 collective-permute-done.1.refs_2_
  21.0 0.7 collective-permute-start.13
  21.7 0.0 collective-permute-done.2.refs_3_
  21.7 1.3 %collective-permute-start.14 = (bf16[32,4096]{1,0:T(8,128)(2,1)S(1)}, bf16[32,4096]{1,0:T(8,128)(2,1)S(1)}, u32[]{:S(2)}, u32[]{:S(2)}) collective-permute-start(bf16[32,4096]{1,0:T(8,128)(2,1)S(1)} %constant_dynamic-update-slice_fusion.refs_0_), channel_id=1, source_target_pairs={{0,2},{1,3},{2,0},{3,1},{4,6},{5,7},{6,4},{7,5},{8,10},{9,11},{10,... | collective-permute-start | bytes 786440 | tf_op jit(solution)/shard_map/ppermute | solution.py:347
  23.0 0.0 collective-permute-done.4.refs_5_
  23.0 1.2 %collective-permute-start.15 = (bf16[32,4096]{1,0:T(8,128)(2,1)S(1)}, bf16[32,4096]{1,0:T(8,128)(2,1)S(1)}, u32[]{:S(2)}, u32[]{:S(2)}) collective-permute-start(bf16[32,4096]{1,0:T(8,128)(2,1)S(1)} %constant_dynamic-update-slice_fusion.refs_0_), channel_id=1, source_target_pairs={{0,3},{1,2},{2,1},{3,0},{4,7},{5,6},{6,5},{7,4},{8,11},{9,10},{10,... | collective-permute-start | bytes 786440 | tf_op jit(solution)/shard_map/ppermute | solution.py:347
  24.1 0.0 collective-permute-done.5.refs_6_
  24.1 0.0 collective-permute-done.6.refs_7_
  24.1 0.0 copy-done
  24.2 5.5 %shard_map.131 = (bf16[128,4096]{1,0:T(8,128)(2,1)S(1)}, bf16[128,1792]{1,0:T(8,128)(2,1)S(1)}, bf16[128,1792]{1,0:T(8,128)(2,1)S(1)}) custom-call(s32[1]{0:T(128)} %bitcast.index_ref, bf16[16,4096]{1,0:T(8,128)(2,1)S(1)} %get-tuple-element.22.refs_0_, bf16[16,4096]{1,0:T(8,128)(2,1)S(1)} %collective-permute-done.refs_1_, ...), custom_call_target="tpu_custom_call" | custom-call | flops 1879048192 | bytes 14680064 | tf_op jit(solution)/shard_map/pallas_call | solution.py:157
  29.7 0.0 slice-done
  29.7 0.0 slice-done.1
  29.7 0.0 slice-done.2
  29.7 0.0 slice-done.3
  29.7 9.4 %shard_map.132 = (bf16[32,4096]{1,0:T(8,128)(2,1)S(1)}, bf16[32,4096]{1,0:T(8,128)(2,1)S(1)}, bf16[32,4096]{1,0:T(8,128)(2,1)S(1)}, bf16[32,4096]{1,0:T(8,128)(2,1)S(1)}) custom-call(s32[1]{0:T(128)} %bitcast.index_ref, bf16[128,1792]{1,0:T(8,128)(2,1)S(1)} %get-tuple-element.26.refs_0_.refs_6_, bf16[128,1792]{1,0:T(8,128)(2,1)S(1)} %get-tuple-element.27.refs_1_.right, ...), custom_call_target="tpu_custom_call" | custom-call | flops 3758096384 | bytes 29360128 | tf_op jit(solution)/shard_map/pallas_call | solution.py:209
  39.1 3.4 %collective-permute-start.7 = (bf16[32,4096]{1,0:T(8,128)(2,1)S(1)}, bf16[32,4096]{1,0:T(8,128)(2,1)S(1)}, u32[]{:S(2)}, u32[]{:S(2)}) collective-permute-start(bf16[32,4096]{1,0:T(8,128)(2,1)S(1)} %get-tuple-element.29), channel_id=1, source_target_pairs={{0,1},{1,0},{2,3},{3,2},{4,5},{5,4},{6,7},{7,6},{8,9},{9,8},{10,11... | collective-permute-start | bytes 786440 | tf_op jit(solution)/shard_map/ppermute | solution.py:347
  42.5 0.0 collective-permute-start.8
  42.5 0.0 collective-permute-done.13.refs_1_
  42.5 1.3 %collective-permute-start.9 = (bf16[32,4096]{1,0:T(8,128)(2,1)S(1)}, bf16[32,4096]{1,0:T(8,128)(2,1)S(1)}, u32[]{:S(2)}, u32[]{:S(2)}) collective-permute-start(bf16[32,4096]{1,0:T(8,128)(2,1)S(1)} %get-tuple-element.31), channel_id=1, source_target_pairs={{0,3},{1,2},{2,1},{3,0},{4,7},{5,6},{6,5},{7,4},{8,11},{9,10},{10,... | collective-permute-start | bytes 786440 | tf_op jit(solution)/shard_map/ppermute | solution.py:347
  43.8 0.0 collective-permute-done.14.refs_2_
  43.8 0.0 collective-permute-done.15.refs_3_
  43.8 12.1 %shard_map.134 = (bf16[1792,4096]{1,0:T(8,128)(2,1)}, bf16[4096,1792]{1,0:T(8,128)(2,1)}, bf16[128,4096]{1,0:T(8,128)(2,1)S(1)}) custom-call(s32[1]{0:T(128)} %bitcast.index_ref, bf16[32,4096]{1,0:T(8,128)(2,1)S(1)} %constant_dynamic-update-slice_fusion.refs_0_, bf16[32,4096]{1,0:T(8,128)(2,1)S(1)} %collective-permute-done.13.refs_1_, ...), custom_call_target="tpu_custom_call" | custom-call | flops 3758096384 | bytes 29360128 | tf_op jit(solution)/shard_map/pallas_call | solution.py:284
  55.8 0.0 collective-permute-done.7
  55.9 0.0 collective-permute-done.8
  55.9 0.0 collective-permute-done.9
  55.9 0.1 add_convert_fusion
  56.1 6.5 %collective-permute-start.10 = (bf16[16,4224]{1,0:T(8,128)(2,1)S(1)}, bf16[16,4224]{1,0:T(8,128)(2,1)S(1)}, u32[]{:S(2)}, u32[]{:S(2)}) collective-permute-start(bf16[16,4224]{1,0:T(8,128)(2,1)S(1)} %pad_maximum_fusion), channel_id=1, source_target_pairs={{8,0},{9,1},{10,2},{11,3},{12,4},{13,5},{14,6},{15,7},{16,8},{17,9... | collective-permute-start | bytes 405512 | tf_op jit(solution)/shard_map/ppermute | solution.py:355
  62.5 3.8 %collective-permute-start.11 = (bf16[16,4096]{1,0:T(8,128)(2,1)S(1)}, bf16[16,4096]{1,0:T(8,128)(2,1)S(1)}, u32[]{:S(2)}, u32[]{:S(2)}) collective-permute-start(bf16[16,4096]{1,0:T(8,128)(2,1)S(1)} %get-tuple-element.40), channel_id=1, source_target_pairs={{8,4},{9,5},{10,6},{11,7},{12,0},{13,1},{14,2},{15,3},{16,12},{17,... | collective-permute-start | bytes 393224 | tf_op jit(solution)/shard_map/ppermute | solution.py:355
  66.4 5.8 %shard_map.135 = bf16[4096,1792]{1,0:T(8,128)(2,1)} custom-call(bf16[128,4096]{1,0:T(8,128)(2,1)S(1)} %get-tuple-element.38.left, bf16[128,1792]{1,0:T(8,128)(2,1)S(1)} %get-tuple-element.27.refs_1_.right), custom_call_target="tpu_custom_call" | custom-call | flops 1879048192 | bytes 14680064 | tf_op jit(solution)/shard_map/pallas_call | solution.py:309
  72.2 2.0 %collective-permute-done.11.sent_ref = bf16[16,4096]{1,0:T(8,128)(2,1)S(1)} collective-permute-done((bf16[16,4096]{1,0:T(8,128)(2,1)S(1)}, bf16[16,4096]{1,0:T(8,128)(2,1)S(1)}, u32[]{:S(2)}, u32[]{:S(2)}) %collective-permute-start.11) | collective-permute-done | bytes 131104 | tf_op jit(solution)/shard_map/ppermute | solution.py:355
  74.2 0.0 collective-permute-done.10.kept_ref
  74.2 1.3 %shard_map.133 = bf16[64,4096]{1,0:T(8,128)(2,1)} custom-call(bf16[16,4224]{1,0:T(8,128)(2,1)S(1)} %collective-permute-done.10.kept_ref, bf16[16,4096]{1,0:T(8,128)(2,1)S(1)} %collective-permute-done.11.sent_ref), custom_call_target="tpu_custom_call" | custom-call | tf_op jit(solution)/shard_map/pallas_call | solution.py:336
  (5 shorter events, 0.1 us)
Async XLA Ops:
  0.6 29.0 %slice-start = ((s8[14680064]{0:T(1024)(128)(4,1)}), s8[4194304]{0:T(1024)(128)(4,1)S(1)}, s32[]{:S(2)}) async-start(s8[14680064]{0:T(1024)(128)(4,1)} %bitcast.23), calls=%async_computation | async-start | bytes 8388608
  0.7 23.5 %copy-start = (bf16[1,1792,4096]{2,1,0:T(8,128)(2,1)S(1)}, bf16[1,1792,4096]{2,1,0:T(8,128)(2,1)}, u32[]{:S(2)}) copy-start(bf16[1,1792,4096]{2,1,0:T(8,128)(2,1)} %param.19) | copy-start | bytes 44040196
  0.7 29.0 %slice-start.1 = ((s8[14680064]{0:T(1024)(128)(4,1)}), s8[4194304]{0:T(1024)(128)(4,1)S(1)}, s32[]{:S(2)}) async-start(s8[14680064]{0:T(1024)(128)(4,1)} %bitcast.23), calls=%async_computation.1 | async-start | bytes 8388608
  0.7 29.0 %slice-start.2 = ((s8[14680064]{0:T(1024)(128)(4,1)}), s8[4194304]{0:T(1024)(128)(4,1)S(1)}, s32[]{:S(2)}) async-start(s8[14680064]{0:T(1024)(128)(4,1)} %bitcast.23), calls=%async_computation.2 | async-start | bytes 8388608
  0.7 29.0 %slice-start.3 = ((s8[14680064]{0:T(1024)(128)(4,1)}), s8[2097152]{0:T(1024)(128)(4,1)S(1)}, s32[]{:S(2)}) async-start(s8[14680064]{0:T(1024)(128)(4,1)} %bitcast.23), calls=%async_computation.3 | async-start | bytes 4194304
  2.5 11.2 %collective-permute-start = (bf16[16,4096]{1,0:T(8,128)(2,1)S(1)}, bf16[16,4096]{1,0:T(8,128)(2,1)S(1)}, u32[]{:S(2)}, u32[]{:S(2)}) collective-permute-start(bf16[16,4096]{1,0:T(8,128)(2,1)S(1)} %get-tuple-element.22.refs_0_), channel_id=1, source_target_pairs={{0,1},{1,0},{2,3},{3,2},{4,5},{5,4},{6,7},{7,6},{8,9},{9,8},{10,11... | collective-permute-start | bytes 393224 | tf_op jit(solution)/shard_map/ppermute | solution.py:347
  4.6 16.4 %collective-permute-start.1 = (bf16[16,4096]{1,0:T(8,128)(2,1)S(1)}, bf16[16,4096]{1,0:T(8,128)(2,1)S(1)}, u32[]{:S(2)}, u32[]{:S(2)}) collective-permute-start(bf16[16,4096]{1,0:T(8,128)(2,1)S(1)} %get-tuple-element.22.refs_0_), channel_id=1, source_target_pairs={{0,2},{1,3},{2,0},{3,1},{4,6},{5,7},{6,4},{7,5},{8,10},{9,11},{10,... | collective-permute-start | bytes 393224 | tf_op jit(solution)/shard_map/ppermute | solution.py:347
  5.9 15.8 %collective-permute-start.2 = (bf16[16,4096]{1,0:T(8,128)(2,1)S(1)}, bf16[16,4096]{1,0:T(8,128)(2,1)S(1)}, u32[]{:S(2)}, u32[]{:S(2)}) collective-permute-start(bf16[16,4096]{1,0:T(8,128)(2,1)S(1)} %get-tuple-element.22.refs_0_), channel_id=1, source_target_pairs={{0,3},{1,2},{2,1},{3,0},{4,7},{5,6},{6,5},{7,4},{8,11},{9,10},{10,... | collective-permute-start | bytes 393224 | tf_op jit(solution)/shard_map/ppermute | solution.py:347
  5.9 7.5 %collective-permute-start.3 = (bf16[16,4096]{1,0:T(8,128)(2,1)S(1)}, bf16[16,4096]{1,0:T(8,128)(2,1)S(1)}, u32[]{:S(2)}, u32[]{:S(2)}) collective-permute-start(bf16[16,4096]{1,0:T(8,128)(2,1)S(1)} %get-tuple-element.23), channel_id=1, source_target_pairs={{0,4},{1,5},{2,6},{3,7},{4,0},{5,1},{6,2},{7,3},{8,12},{9,13},{10,... | collective-permute-start | bytes 393224 | tf_op jit(solution)/shard_map/ppermute | solution.py:347
  8.3 8.8 %collective-permute-start.12 = (bf16[16,4096]{1,0:T(8,128)(2,1)S(1)}, bf16[16,4096]{1,0:T(8,128)(2,1)S(1)}, u32[]{:S(2)}, u32[]{:S(2)}) collective-permute-start(bf16[16,4096]{1,0:T(8,128)(2,1)S(1)} %get-tuple-element.34), channel_id=1, source_target_pairs={{0,4},{1,5},{2,6},{3,7},{4,0},{5,1},{6,2},{7,3},{8,12},{9,13},{10,... | collective-permute-start | bytes 393224 | tf_op jit(solution)/shard_map/ppermute | solution.py:347
  13.4 9.6 %collective-permute-start.4 = (bf16[16,4096]{1,0:T(8,128)(2,1)S(1)}, bf16[16,4096]{1,0:T(8,128)(2,1)S(1)}, u32[]{:S(2)}, u32[]{:S(2)}) collective-permute-start(bf16[16,4096]{1,0:T(8,128)(2,1)S(1)} %collective-permute-done.3.refs_4_), channel_id=1, source_target_pairs={{0,1},{1,0},{2,3},{3,2},{4,5},{5,4},{6,7},{7,6},{8,9},{9,8},{10,11... | collective-permute-start | bytes 393224 | tf_op jit(solution)/shard_map/ppermute | solution.py:347
  13.6 10.5 %collective-permute-start.5 = (bf16[16,4096]{1,0:T(8,128)(2,1)S(1)}, bf16[16,4096]{1,0:T(8,128)(2,1)S(1)}, u32[]{:S(2)}, u32[]{:S(2)}) collective-permute-start(bf16[16,4096]{1,0:T(8,128)(2,1)S(1)} %collective-permute-done.3.refs_4_), channel_id=1, source_target_pairs={{0,2},{1,3},{2,0},{3,1},{4,6},{5,7},{6,4},{7,5},{8,10},{9,11},{10,... | collective-permute-start | bytes 393224 | tf_op jit(solution)/shard_map/ppermute | solution.py:347
  17.1 7.0 %collective-permute-start.6 = (bf16[16,4096]{1,0:T(8,128)(2,1)S(1)}, bf16[16,4096]{1,0:T(8,128)(2,1)S(1)}, u32[]{:S(2)}, u32[]{:S(2)}) collective-permute-start(bf16[16,4096]{1,0:T(8,128)(2,1)S(1)} %collective-permute-done.3.refs_4_), channel_id=1, source_target_pairs={{0,3},{1,2},{2,1},{3,0},{4,7},{5,6},{6,5},{7,4},{8,11},{9,10},{10,... | collective-permute-start | bytes 393224 | tf_op jit(solution)/shard_map/ppermute | solution.py:347
  21.0 21.5 %collective-permute-start.13 = (bf16[32,4096]{1,0:T(8,128)(2,1)S(1)}, bf16[32,4096]{1,0:T(8,128)(2,1)S(1)}, u32[]{:S(2)}, u32[]{:S(2)}) collective-permute-start(bf16[32,4096]{1,0:T(8,128)(2,1)S(1)} %constant_dynamic-update-slice_fusion.refs_0_), channel_id=1, source_target_pairs={{0,1},{1,0},{2,3},{3,2},{4,5},{5,4},{6,7},{7,6},{8,9},{9,8},{10,11... | collective-permute-start | bytes 786440 | tf_op jit(solution)/shard_map/ppermute | solution.py:347
  21.7 22.1 %collective-permute-start.14 = (bf16[32,4096]{1,0:T(8,128)(2,1)S(1)}, bf16[32,4096]{1,0:T(8,128)(2,1)S(1)}, u32[]{:S(2)}, u32[]{:S(2)}) collective-permute-start(bf16[32,4096]{1,0:T(8,128)(2,1)S(1)} %constant_dynamic-update-slice_fusion.refs_0_), channel_id=1, source_target_pairs={{0,2},{1,3},{2,0},{3,1},{4,6},{5,7},{6,4},{7,5},{8,10},{9,11},{10,... | collective-permute-start | bytes 786440 | tf_op jit(solution)/shard_map/ppermute | solution.py:347
  23.0 20.8 %collective-permute-start.15 = (bf16[32,4096]{1,0:T(8,128)(2,1)S(1)}, bf16[32,4096]{1,0:T(8,128)(2,1)S(1)}, u32[]{:S(2)}, u32[]{:S(2)}) collective-permute-start(bf16[32,4096]{1,0:T(8,128)(2,1)S(1)} %constant_dynamic-update-slice_fusion.refs_0_), channel_id=1, source_target_pairs={{0,3},{1,2},{2,1},{3,0},{4,7},{5,6},{6,5},{7,4},{8,11},{9,10},{10,... | collective-permute-start | bytes 786440 | tf_op jit(solution)/shard_map/ppermute | solution.py:347
  39.1 16.7 %collective-permute-start.7 = (bf16[32,4096]{1,0:T(8,128)(2,1)S(1)}, bf16[32,4096]{1,0:T(8,128)(2,1)S(1)}, u32[]{:S(2)}, u32[]{:S(2)}) collective-permute-start(bf16[32,4096]{1,0:T(8,128)(2,1)S(1)} %get-tuple-element.29), channel_id=1, source_target_pairs={{0,1},{1,0},{2,3},{3,2},{4,5},{5,4},{6,7},{7,6},{8,9},{9,8},{10,11... | collective-permute-start | bytes 786440 | tf_op jit(solution)/shard_map/ppermute | solution.py:347
  42.5 13.4 %collective-permute-start.8 = (bf16[32,4096]{1,0:T(8,128)(2,1)S(1)}, bf16[32,4096]{1,0:T(8,128)(2,1)S(1)}, u32[]{:S(2)}, u32[]{:S(2)}) collective-permute-start(bf16[32,4096]{1,0:T(8,128)(2,1)S(1)} %get-tuple-element.30), channel_id=1, source_target_pairs={{0,2},{1,3},{2,0},{3,1},{4,6},{5,7},{6,4},{7,5},{8,10},{9,11},{10,... | collective-permute-start | bytes 786440 | tf_op jit(solution)/shard_map/ppermute | solution.py:347
  42.5 13.4 %collective-permute-start.9 = (bf16[32,4096]{1,0:T(8,128)(2,1)S(1)}, bf16[32,4096]{1,0:T(8,128)(2,1)S(1)}, u32[]{:S(2)}, u32[]{:S(2)}) collective-permute-start(bf16[32,4096]{1,0:T(8,128)(2,1)S(1)} %get-tuple-element.31), channel_id=1, source_target_pairs={{0,3},{1,2},{2,1},{3,0},{4,7},{5,6},{6,5},{7,4},{8,11},{9,10},{10,... | collective-permute-start | bytes 786440 | tf_op jit(solution)/shard_map/ppermute | solution.py:347
  56.1 18.1 %collective-permute-start.10 = (bf16[16,4224]{1,0:T(8,128)(2,1)S(1)}, bf16[16,4224]{1,0:T(8,128)(2,1)S(1)}, u32[]{:S(2)}, u32[]{:S(2)}) collective-permute-start(bf16[16,4224]{1,0:T(8,128)(2,1)S(1)} %pad_maximum_fusion), channel_id=1, source_target_pairs={{8,0},{9,1},{10,2},{11,3},{12,4},{13,5},{14,6},{15,7},{16,8},{17,9... | collective-permute-start | bytes 405512 | tf_op jit(solution)/shard_map/ppermute | solution.py:355
  62.5 11.6 %collective-permute-start.11 = (bf16[16,4096]{1,0:T(8,128)(2,1)S(1)}, bf16[16,4096]{1,0:T(8,128)(2,1)S(1)}, u32[]{:S(2)}, u32[]{:S(2)}) collective-permute-start(bf16[16,4096]{1,0:T(8,128)(2,1)S(1)} %get-tuple-element.40), channel_id=1, source_target_pairs={{8,4},{9,5},{10,6},{11,7},{12,0},{13,1},{14,2},{15,3},{16,12},{17,... | collective-permute-start | bytes 393224 | tf_op jit(solution)/shard_map/ppermute | solution.py:355
where the time goes:
time: 75.6 us; the launch traced here: 75.5 us
  Pallas kernels  38.3 us (51%)
  starting transfers between devices  31.5 us (42%)
  waiting for transfers between devices  4.59 us (6%)
  between operations  0.87 us (1%)
    ppermute x14, starting transfers between devices, to_partner(): return lax.ppermute(value, 'expert', [(i, i ^ m) for i in range(peers)])  21.2 us
    pallas_call x1, Pallas kernels, first_stage(): pl.pallas_call(functools.partial(first_kernel, capacity, pairs), in_specs...  12.1 us
    ppermute x2, starting transfers between devices, to_behind(): return lax.ppermute(value, ('section', 'expert'), pairs)  10.3 us
    pallas_call x1, Pallas kernels, part_stage(): pl.pallas_call(functools.partial(part_kernel, capacity, group, step), in_...  9.38 us
    pallas_call x1, Pallas kernels, second_stage(): pl.pallas_call(second_kernel, in_specs=[vmem()] * 2, out_specs=hbm(), out...  5.79 us
    pallas_call x1, Pallas kernels, hidden_stage(): pl.pallas_call(functools.partial(hidden_kernel, capacity, pairs), in_spec...  5.53 us
    ppermute x14, waiting for transfers between devices, to_partner(): return lax.ppermute(value, 'expert', [(i, i ^ m) for i in range(peers)])  2.61 us
    pallas_call x1, Pallas kernels, saved_stage(): pl.pallas_call(saved_kernel, in_specs=[hbm()] * 2, out_specs=[vmem()] * 3...  2.48 us
  transfers between devices with their start and end apart: 16, of which 2 were waited for; matrix products, arithmetic and copies ran while one was open for 0% of the time, Pallas kernels for 47%

commit v1 on v0

--- a/solution.py
+++ b/solution.py
@@ -10,6 +10,8 @@
 
 EXPERTS = 8
 E_WIN = 2
+EARLY = 2
+GRANT = 24
 BF16 = jnp.bfloat16
 F32 = jnp.float32
 NT = (((1,), (1,)), ((), ()))
@@ -167,10 +169,10 @@
     )(index, *blocks, act, slope, w_down)
 
 
-def part_kernel(capacity, group, step, index_ref, *refs):
-    gate_grad, up_grad, w_gate, up_hbm = refs[:4]
-    outs = refs[4 : 4 + group]
-    half, stage, w_up, sems = refs[4 + group :]
+def part_kernel(capacity, group, step, early, index_ref, *refs):
+    gate_grad, up_grad, w_gate, hidden, rows_grad, up_hbm = refs[:6]
+    outs, down = refs[6 : 6 + group], refs[6 + group]
+    half, stage, w_up, sems, stage_down, sems_down = refs[7 + group :]
     index = index_ref[0]
     cuts = sems.shape[0]
     width = w_gate.shape[0]
@@ -183,6 +185,7 @@
     ]
     for copy in ahead:
         copy.start()
+    leaving = write_out(hidden, rows_grad, down, stage_down, sems_down, 0, early)
     for start in range(0, width, step):
         some = slice(start, start + step)
         half[some, :] = lax.dot_general(
@@ -200,28 +203,38 @@
         source = pl.multiple_of(jnp.bitwise_xor(index, m) * capacity, capacity)
         start = m // group * capacity
         outs[m % group][start : start + capacity, :] = stage[pl.ds(source, capacity), :]
-
-
-def part_stage(index, gate_grad, up_grad, w_gate, w_up, capacity, group):
+    for copy in leaving:
+        copy.wait()
+
+
+def down_slabs(units):
+    slab = piece(units, 256)
+    return slab, EARLY * (units // slab) // 7
+
+
+def part_stage(index, gate_grad, up_grad, w_gate, hidden, rows_grad, w_up, capacity, group):
     width, units = w_gate.shape
     total = gate_grad.shape[0]
     step = piece(width, 512)
-    return pl.pallas_call(
-        functools.partial(part_kernel, capacity, group, step),
-        in_specs=[smem()] + [vmem()] * 3 + [hbm()],
-        out_specs=[vmem()] * group,
-        out_shape=[like((2 * capacity, width))] * group,
+    slab, early = down_slabs(units)
+    return pl.pallas_call(
+        functools.partial(part_kernel, capacity, group, step, early),
+        in_specs=[smem()] + [vmem()] * 5 + [hbm()],
+        out_specs=[vmem()] * group + [hbm()],
+        out_shape=[like((2 * capacity, width))] * group + [like((units, width))],
         scratch_shapes=[
             pltpu.VMEM((width, total), F32),
             pltpu.VMEM((total, width), BF16),
             pltpu.VMEM((width, units), BF16),
             pltpu.SemaphoreType.DMA((4,)),
+            pltpu.VMEM((max(early, 1) * slab, width), BF16),
+            pltpu.SemaphoreType.DMA((max(early, 1),)),
         ],
-        compiler_params=params(24),
+        compiler_params=params(GRANT),
         cost_estimate=pl.CostEstimate(
             flops=4 * total * units * width, bytes_accessed=4 * units * width, transcendentals=0
         ),
-    )(index, gate_grad, up_grad, w_gate, w_up)
+    )(index, gate_grad, up_grad, w_gate, hidden, rows_grad, w_up)
 
 
 def land(capacity, pairs, index, blocks, rows, sems):
@@ -239,16 +252,17 @@
     return copies
 
 
-def write_out(left, right, out, stage, sems):
-    step = out.shape[0] // sems.shape[0]
+def write_out(left, right, out, stage, sems, first=0, count=None):
+    count = sems.shape[0] if count is None else count
+    step = stage.shape[0] // max(count, 1)
     copies = []
-    for n in range(sems.shape[0]):
-        some = slice(n * step, (n + 1) * step)
-        stage[some, :] = lax.dot_general(
+    for n in range(count):
+        some = slice(first + n * step, first + (n + 1) * step)
+        stage[n * step : (n + 1) * step, :] = lax.dot_general(
             left[:, some], right[...], TN, preferred_element_type=F32
         ).astype(BF16)
         copy = pltpu.make_async_copy(
-            stage.at[pl.ds(n * step, step)], out.at[pl.ds(n * step, step)], sems.at[n]
+            stage.at[pl.ds(n * step, step)], out.at[pl.ds(first + n * step, step)], sems.at[n]
         )
         copy.start()
         copies.append(copy)
@@ -257,12 +271,13 @@
 
 def first_kernel(capacity, pairs, index_ref, *refs):
     blocks = refs[: len(pairs)]
-    hidden, rows_grad, gate_grad, down, gate, rows_in = refs[len(pairs) : len(pairs) + 6]
-    stage_down, stage_gate, sems_down, sems_gate, block_sems = refs[len(pairs) + 6 :]
+    hidden, rows_grad, gate_grad, _, down, gate, rows_in = refs[len(pairs) : len(pairs) + 7]
+    stage_down, stage_gate, sems_down, sems_gate, block_sems = refs[len(pairs) + 7 :]
+    begun = down.shape[0] - stage_down.shape[0]
     copies = land(capacity, pairs, index_ref[0], blocks, rows_in, block_sems)
     for copy in copies:
         copy.start()
-    left = write_out(hidden, rows_grad, down, stage_down, sems_down)
+    left = write_out(hidden, rows_grad, down, stage_down, sems_down, begun)
     for copy in copies:
         copy.wait()
     left += write_out(rows_in, gate_grad, gate, stage_gate, sems_gate)
@@ -278,24 +293,27 @@
     )
 
 
-def first_stage(index, blocks, pairs, hidden, rows_grad, gate_grad, capacity):
+def first_stage(index, blocks, pairs, hidden, rows_grad, gate_grad, down, capacity):
     total, units = hidden.shape
     width = rows_grad.shape[1]
+    slab, early = down_slabs(units)
+    late = units // slab - early
     return pl.pallas_call(
         functools.partial(first_kernel, capacity, pairs),
-        in_specs=[smem()] + [anywhere()] * len(blocks) + [vmem()] * 3,
+        in_specs=[smem()] + [anywhere()] * len(blocks) + [vmem()] * 3 + [hbm()],
         out_specs=[hbm(), hbm(), vmem()],
         out_shape=[like((units, width)), like((width, units)), like((total, width))],
         scratch_shapes=[
-            pltpu.VMEM((units, width), BF16),
+            pltpu.VMEM((late * slab, width), BF16),
             pltpu.VMEM((width, units), BF16),
-            pltpu.SemaphoreType.DMA((units // piece(units, 256),)),
+            pltpu.SemaphoreType.DMA((late,)),
             pltpu.SemaphoreType.DMA((width // piece(width, 512),)),
             pltpu.SemaphoreType.DMA((total // capacity,)),
         ],
+        input_output_aliases={4 + len(blocks): 0},
         compiler_params=params(36),
         cost_estimate=weight_cost(2, total, units, width),
-    )(index, *blocks, hidden, rows_grad, gate_grad)
+    )(index, *blocks, hidden, rows_grad, gate_grad, down)
 
 
 def second_kernel(left, right, out, stage, sems):
@@ -392,13 +410,21 @@
     )
     both = jnp.concatenate([in_own, in_crossed], axis=0)
     in_blocks = [both] + [to_partner(both, m) for m in range(1, group)]
-    parts = part_stage(
-        index, gate_grad, up_grad, w_gate[0], stay(w_up[0]), capacity, group
+    *parts, grad_down = part_stage(
+        index,
+        gate_grad,
+        up_grad,
+        w_gate[0],
+        hidden,
+        rows_grad,
+        stay(w_up[0]),
+        capacity,
+        group,
     )
     returned = [to_partner(parts[m], m) for m in range(1, group)]
     pairs = [(m, m + group) for m in range(group)]
     grad_down, grad_gate, rows_in = first_stage(
-        index, in_blocks, pairs, hidden, rows_grad, gate_grad, capacity
+        index, in_blocks, pairs, hidden, rows_grad, gate_grad, grad_down, capacity
     )
     summed = parts[0].astype(F32)
     for part in returned:

time: 75.6 us -> 78.1 us (1.033)
  starting transfers between devices: 31.5 us -> 34.6 us
    ppermute x14, starting transfers between devices: 21.2 us -> 24.8 us  [to_partner(): return lax.ppermute(value, 'expert', [(i, i ^ m) for i in range(peers)])]
    ppermute x14, waiting for transfers between devices: 2.61 us -> 4.68 us  [to_partner(): return lax.ppermute(value, 'expert', [(i, i ^ m) for i in range(peers)])]
    ppermute x2, waiting for transfers between devices: 1.98 us -> 0.01 us  [to_behind(): return lax.ppermute(value, ('section', 'expert'), pairs)]
    pallas_call x1, Pallas kernels: 12.1 us -> 10.8 us  [first_stage(): pl.pallas_call(functools.partial(first_kernel, capacity, pairs), in_specs...]
  transfers between devices with their start and end apart: 16 -> 16, of which waited for: 2 -> 2; matrix products, arithmetic and copies ran while one was open for 0% -> 0% of each run, Pallas kernels for 47% -> 44%
where the time goes in v1:
time: 78.1 us; the launch traced here: 78 us
  Pallas kernels  37.6 us (48%)
  starting transfers between devices  34.6 us (44%)
  waiting for transfers between devices  4.68 us (6%)
  between operations  0.89 us (1%)
    ppermute x14, starting transfers between devices, to_partner(): return lax.ppermute(value, 'expert', [(i, i ^ m) for i in range(peers)])  24.8 us
    pallas_call x1, Pallas kernels, first_stage(): pl.pallas_call(functools.partial(first_kernel, capacity, pairs), in_specs...  10.8 us
    pallas_call x1, Pallas kernels, part_stage(): pl.pallas_call(functools.partial(part_kernel, capacity, group, step, earl...  9.92 us
    ppermute x2, starting transfers between devices, to_behind(): return lax.ppermute(value, ('section', 'expert'), pairs)  9.85 us
    pallas_call x1, Pallas kernels, second_stage(): pl.pallas_call(second_kernel, in_specs=[vmem()] * 2, out_specs=hbm(), out...  5.79 us
    pallas_call x1, Pallas kernels, hidden_stage(): pl.pallas_call(functools.partial(hidden_kernel, capacity, pairs), in_spec...  5.49 us
    ppermute x14, waiting for transfers between devices, to_partner(): return lax.ppermute(value, 'expert', [(i, i ^ m) for i in range(peers)])  4.68 us
    pallas_call x1, Pallas kernels, saved_stage(): pl.pallas_call(saved_kernel, in_specs=[hbm()] * 2, out_specs=[vmem()] * 3...  2.48 us
  transfers between devices with their start and end apart: 16, of which 2 were waited for; matrix products, arithmetic and copies ran while one was open for 0% of the time, Pallas kernels for 44%

profile of v1, /device:TPU:1, one launch (start us, length us, event | category | flops | bytes accessed | tf_op | source)
XLA Modules:
  0.0 78.0 jit_solution(9212468145175381266)
XLA Ops:
  0.6 0.0 slice-start
  0.7 0.0 copy-start
  0.7 0.0 slice-start.1
  0.7 0.0 slice-start.2
  0.7 0.0 slice-start.3
  0.7 1.7 %shard_map.129 = (bf16[16,4096]{1,0:T(8,128)(2,1)S(1)}, bf16[16,4096]{1,0:T(8,128)(2,1)S(1)}, bf16[16,4096]{1,0:T(8,128)(2,1)S(1)}, bf16[16,4096]{1,0:T(8,128)(2,1)S(1)}, bf16[16,128]{1,0:T(8,128)(2,1)S(1)}) custom-call(s32[1]{0:T(128)} %bitcast.1.half_ref, s32[2,64]{1,0:T(2,128)} %bitcast.35, s32[2,64]{1,0:T(2,128)} %bitcast.36, s32[2,64]{1,0:T(2,128)} %bitcast.37, ...), custom_call_target="tpu_custom_call" | custom-call | flops 68719476736 | bytes 1572864 | tf_op jit(solution)/shard_map/pallas_call | solution.py:93
  2.5 3.1 %collective-permute-start.2 = (bf16[16,4096]{1,0:T(8,128)(2,1)S(1)}, bf16[16,4096]{1,0:T(8,128)(2,1)S(1)}, u32[]{:S(2)}, u32[]{:S(2)}) collective-permute-start(bf16[16,4096]{1,0:T(8,128)(2,1)S(1)} %get-tuple-element.23.refs_0_), channel_id=1, source_target_pairs={{0,3},{1,2},{2,1},{3,0},{4,7},{5,6},{6,5},{7,4},{8,11},{9,10},{10,... | collective-permute-start | bytes 393224 | tf_op jit(solution)/shard_map/ppermute | solution.py:365
  5.6 0.2 collective-permute-start.1
  5.8 0.2 collective-permute-start
  6.0 2.3 %collective-permute-start.3 = (bf16[16,4096]{1,0:T(8,128)(2,1)S(1)}, bf16[16,4096]{1,0:T(8,128)(2,1)S(1)}, u32[]{:S(2)}, u32[]{:S(2)}) collective-permute-start(bf16[16,4096]{1,0:T(8,128)(2,1)S(1)} %get-tuple-element.24), channel_id=1, source_target_pairs={{0,4},{1,5},{2,6},{3,7},{4,0},{5,1},{6,2},{7,3},{8,12},{9,13},{10,... | collective-permute-start | bytes 393224 | tf_op jit(solution)/shard_map/ppermute | solution.py:365
  8.3 0.0 collective-permute-start.12
  8.3 2.5 %shard_map.130 = (bf16[128,1792]{1,0:T(8,128)(2,1)S(1)}, f32[128,1792]{1,0:T(8,128)S(1)}, f32[128,1792]{1,0:T(8,128)S(1)}) custom-call(bf16[128,1792]{1,0:T(8,128)(2,1)} %bitcast.30, bf16[128,1792]{1,0:T(8,128)(2,1)} %bitcast.31), custom_call_target="tpu_custom_call" | custom-call | flops 3670016 | bytes 3211264 | tf_op jit(solution)/shard_map/pallas_call | solution.py:127
  10.8 2.6 %collective-permute-done.3.refs_4_ = bf16[16,4096]{1,0:T(8,128)(2,1)S(1)} collective-permute-done((bf16[16,4096]{1,0:T(8,128)(2,1)S(1)}, bf16[16,4096]{1,0:T(8,128)(2,1)S(1)}, u32[]{:S(2)}, u32[]{:S(2)}) %collective-permute-start.3) | collective-permute-done | bytes 131104 | tf_op jit(solution)/shard_map/ppermute | solution.py:365
  13.4 3.1 %collective-permute-start.6 = (bf16[16,4096]{1,0:T(8,128)(2,1)S(1)}, bf16[16,4096]{1,0:T(8,128)(2,1)S(1)}, u32[]{:S(2)}, u32[]{:S(2)}) collective-permute-start(bf16[16,4096]{1,0:T(8,128)(2,1)S(1)} %collective-permute-done.3.refs_4_), channel_id=1, source_target_pairs={{0,3},{1,2},{2,1},{3,0},{4,7},{5,6},{6,5},{7,4},{8,11},{9,10},{10,... | collective-permute-start | bytes 393224 | tf_op jit(solution)/shard_map/ppermute | solution.py:365
  16.5 0.0 collective-permute-done.12
  16.5 2.9 %collective-permute-start.5 = (bf16[16,4096]{1,0:T(8,128)(2,1)S(1)}, bf16[16,4096]{1,0:T(8,128)(2,1)S(1)}, u32[]{:S(2)}, u32[]{:S(2)}) collective-permute-start(bf16[16,4096]{1,0:T(8,128)(2,1)S(1)} %collective-permute-done.3.refs_4_), channel_id=1, source_target_pairs={{0,2},{1,3},{2,0},{3,1},{4,6},{5,7},{6,4},{7,5},{8,10},{9,11},{10,... | collective-permute-start | bytes 393224 | tf_op jit(solution)/shard_map/ppermute | solution.py:365
  19.5 0.0 collective-permute-done.2.refs_3_
  19.5 2.1 %collective-permute-start.4 = (bf16[16,4096]{1,0:T(8,128)(2,1)S(1)}, bf16[16,4096]{1,0:T(8,128)(2,1)S(1)}, u32[]{:S(2)}, u32[]{:S(2)}) collective-permute-start(bf16[16,4096]{1,0:T(8,128)(2,1)S(1)} %collective-permute-done.3.refs_4_), channel_id=1, source_target_pairs={{0,1},{1,0},{2,3},{3,2},{4,5},{5,4},{6,7},{7,6},{8,9},{9,8},{10,11... | collective-permute-start | bytes 393224 | tf_op jit(solution)/shard_map/ppermute | solution.py:365
  21.6 0.0 collective-permute-done.1.refs_2_
  21.6 1.2 %collective-permute-start.15 = (bf16[32,4096]{1,0:T(8,128)(2,1)S(1)}, bf16[32,4096]{1,0:T(8,128)(2,1)S(1)}, u32[]{:S(2)}, u32[]{:S(2)}) collective-permute-start(bf16[32,4096]{1,0:T(8,128)(2,1)S(1)} %constant_dynamic-update-slice_fusion.refs_0_), channel_id=1, source_target_pairs={{0,3},{1,2},{2,1},{3,0},{4,7},{5,6},{6,5},{7,4},{8,11},{9,10},{10,... | collective-permute-start | bytes 786440 | tf_op jit(solution)/shard_map/ppermute | solution.py:365
  22.8 0.0 collective-permute-done.refs_1_
  22.8 0.4 collective-permute-start.14
  23.2 0.0 collective-permute-done.6.refs_7_
  23.2 1.2 %collective-permute-start.13 = (bf16[32,4096]{1,0:T(8,128)(2,1)S(1)}, bf16[32,4096]{1,0:T(8,128)(2,1)S(1)}, u32[]{:S(2)}, u32[]{:S(2)}) collective-permute-start(bf16[32,4096]{1,0:T(8,128)(2,1)S(1)} %constant_dynamic-update-slice_fusion.refs_0_), channel_id=1, source_target_pairs={{0,1},{1,0},{2,3},{3,2},{4,5},{5,4},{6,7},{7,6},{8,9},{9,8},{10,11... | collective-permute-start | bytes 786440 | tf_op jit(solution)/shard_map/ppermute | solution.py:365
  24.4 0.0 collective-permute-done.5.refs_6_
  24.4 2.1 %collective-permute-done.4.refs_5_ = bf16[16,4096]{1,0:T(8,128)(2,1)S(1)} collective-permute-done((bf16[16,4096]{1,0:T(8,128)(2,1)S(1)}, bf16[16,4096]{1,0:T(8,128)(2,1)S(1)}, u32[]{:S(2)}, u32[]{:S(2)}) %collective-permute-start.4) | collective-permute-done | bytes 131104 | tf_op jit(solution)/shard_map/ppermute | solution.py:365
  26.5 0.0 copy-done
  26.5 5.5 %shard_map.131 = (bf16[128,4096]{1,0:T(8,128)(2,1)S(1)}, bf16[128,1792]{1,0:T(8,128)(2,1)S(1)}, bf16[128,1792]{1,0:T(8,128)(2,1)S(1)}) custom-call(s32[1]{0:T(128)} %bitcast.index_ref, bf16[16,4096]{1,0:T(8,128)(2,1)S(1)} %get-tuple-element.23.refs_0_, bf16[16,4096]{1,0:T(8,128)(2,1)S(1)} %collective-permute-done.refs_1_, ...), custom_call_target="tpu_custom_call" | custom-call | flops 1879048192 | bytes 14680064 | tf_op jit(solution)/shard_map/pallas_call | solution.py:159
  32.0 0.0 slice-done
  32.0 0.0 slice-done.1
  32.0 0.0 slice-done.2
  32.0 0.0 slice-done.3
  32.0 9.9 %shard_map.132 = (bf16[32,4096]{1,0:T(8,128)(2,1)S(1)}, bf16[32,4096]{1,0:T(8,128)(2,1)S(1)}, bf16[32,4096]{1,0:T(8,128)(2,1)S(1)}, bf16[32,4096]{1,0:T(8,128)(2,1)S(1)}, bf16[1792,4096]{1,0:T(8,128)(2,1)}) custom-call(s32[1]{0:T(128)} %bitcast.index_ref, bf16[128,1792]{1,0:T(8,128)(2,1)S(1)} %get-tuple-element.27.refs_0_.refs_6_, ...), custom_call_target="tpu_custom_call" | custom-call | flops 3758096384 | bytes 29360128 | tf_op jit(solution)/shard_map/pallas_call | solution.py:220
  41.9 2.8 %collective-permute-start.7 = (bf16[32,4096]{1,0:T(8,128)(2,1)S(1)}, bf16[32,4096]{1,0:T(8,128)(2,1)S(1)}, u32[]{:S(2)}, u32[]{:S(2)}) collective-permute-start(bf16[32,4096]{1,0:T(8,128)(2,1)S(1)} %get-tuple-element.32), channel_id=1, source_target_pairs={{0,1},{1,0},{2,3},{3,2},{4,5},{5,4},{6,7},{7,6},{8,9},{9,8},{10,11... | collective-permute-start | bytes 786440 | tf_op jit(solution)/shard_map/ppermute | solution.py:365
  44.7 5.2 %collective-permute-start.8 = (bf16[32,4096]{1,0:T(8,128)(2,1)S(1)}, bf16[32,4096]{1,0:T(8,128)(2,1)S(1)}, u32[]{:S(2)}, u32[]{:S(2)}) collective-permute-start(bf16[32,4096]{1,0:T(8,128)(2,1)S(1)} %get-tuple-element.33), channel_id=1, source_target_pairs={{0,2},{1,3},{2,0},{3,1},{4,6},{5,7},{6,4},{7,5},{8,10},{9,11},{10,... | collective-permute-start | bytes 786440 | tf_op jit(solution)/shard_map/ppermute | solution.py:365
  49.9 0.0 collective-permute-done.15.refs_3_
  49.9 0.0 collective-permute-start.9
  49.9 0.0 collective-permute-done.14.refs_2_
  49.9 0.0 collective-permute-done.13.refs_1_
  49.9 10.8 %shard_map.134 = (bf16[1792,4096]{1,0:T(8,128)(2,1)}, bf16[4096,1792]{1,0:T(8,128)(2,1)}, bf16[128,4096]{1,0:T(8,128)(2,1)S(1)}) custom-call(s32[1]{0:T(128)} %bitcast.index_ref, bf16[32,4096]{1,0:T(8,128)(2,1)S(1)} %constant_dynamic-update-slice_fusion.refs_0_, ...), custom_call_target="tpu_custom_call", output_to_operand_aliasing={{0}: (8, {})} | custom-call | flops 3758096384 | bytes 29360128 | tf_op jit(solution)/shard_map/pallas_call | solution.py:301
  60.8 0.0 collective-permute-done.7
  60.8 0.0 collective-permute-done.8
  60.8 0.0 collective-permute-done.9
  60.8 0.1 add_convert_fusion
  61.0 7.9 %collective-permute-start.11 = (bf16[16,4096]{1,0:T(8,128)(2,1)S(1)}, bf16[16,4096]{1,0:T(8,128)(2,1)S(1)}, u32[]{:S(2)}, u32[]{:S(2)}) collective-permute-start(bf16[16,4096]{1,0:T(8,128)(2,1)S(1)} %get-tuple-element.42), channel_id=1, source_target_pairs={{8,4},{9,5},{10,6},{11,7},{12,0},{13,1},{14,2},{15,3},{16,12},{17,... | collective-permute-start | bytes 393224 | tf_op jit(solution)/shard_map/ppermute | solution.py:373
  68.9 1.9 %collective-permute-start.10 = (bf16[16,4224]{1,0:T(8,128)(2,1)S(1)}, bf16[16,4224]{1,0:T(8,128)(2,1)S(1)}, u32[]{:S(2)}, u32[]{:S(2)}) collective-permute-start(bf16[16,4224]{1,0:T(8,128)(2,1)S(1)} %pad_maximum_fusion), channel_id=1, source_target_pairs={{8,0},{9,1},{10,2},{11,3},{12,4},{13,5},{14,6},{15,7},{16,8},{17,9... | collective-permute-start | bytes 405512 | tf_op jit(solution)/shard_map/ppermute | solution.py:373
  70.8 5.8 %shard_map.135 = bf16[4096,1792]{1,0:T(8,128)(2,1)} custom-call(bf16[128,4096]{1,0:T(8,128)(2,1)S(1)} %get-tuple-element.40.left, bf16[128,1792]{1,0:T(8,128)(2,1)S(1)} %get-tuple-element.28.refs_1_.right), custom_call_target="tpu_custom_call" | custom-call | flops 1879048192 | bytes 14680064 | tf_op jit(solution)/shard_map/pallas_call | solution.py:327
  76.6 0.0 collective-permute-done.11.sent_ref
  76.7 0.0 collective-permute-done.10.kept_ref
  76.7 1.3 %shard_map.133 = bf16[64,4096]{1,0:T(8,128)(2,1)} custom-call(bf16[16,4224]{1,0:T(8,128)(2,1)S(1)} %collective-permute-done.10.kept_ref, bf16[16,4096]{1,0:T(8,128)(2,1)S(1)} %collective-permute-done.11.sent_ref), custom_call_target="tpu_custom_call" | custom-call | tf_op jit(solution)/shard_map/pallas_call | solution.py:354
  (5 shorter events, 0.1 us)
Async XLA Ops:
  0.6 31.3 %slice-start = ((s8[14680064]{0:T(1024)(128)(4,1)}), s8[4194304]{0:T(1024)(128)(4,1)S(1)}, s32[]{:S(2)}) async-start(s8[14680064]{0:T(1024)(128)(4,1)} %bitcast.23), calls=%async_computation | async-start | bytes 8388608
  0.7 25.8 %copy-start = (bf16[1,1792,4096]{2,1,0:T(8,128)(2,1)S(1)}, bf16[1,1792,4096]{2,1,0:T(8,128)(2,1)}, u32[]{:S(2)}) copy-start(bf16[1,1792,4096]{2,1,0:T(8,128)(2,1)} %param.19) | copy-start | bytes 44040196
  0.7 31.3 %slice-start.1 = ((s8[14680064]{0:T(1024)(128)(4,1)}), s8[4194304]{0:T(1024)(128)(4,1)S(1)}, s32[]{:S(2)}) async-start(s8[14680064]{0:T(1024)(128)(4,1)} %bitcast.23), calls=%async_computation.1 | async-start | bytes 8388608
  0.7 31.3 %slice-start.2 = ((s8[14680064]{0:T(1024)(128)(4,1)}), s8[4194304]{0:T(1024)(128)(4,1)S(1)}, s32[]{:S(2)}) async-start(s8[14680064]{0:T(1024)(128)(4,1)} %bitcast.23), calls=%async_computation.2 | async-start | bytes 8388608
  0.7 31.3 %slice-start.3 = ((s8[14680064]{0:T(1024)(128)(4,1)}), s8[2097152]{0:T(1024)(128)(4,1)S(1)}, s32[]{:S(2)}) async-start(s8[14680064]{0:T(1024)(128)(4,1)} %bitcast.23), calls=%async_computation.3 | async-start | bytes 4194304
  2.5 17.0 %collective-permute-start.2 = (bf16[16,4096]{1,0:T(8,128)(2,1)S(1)}, bf16[16,4096]{1,0:T(8,128)(2,1)S(1)}, u32[]{:S(2)}, u32[]{:S(2)}) collective-permute-start(bf16[16,4096]{1,0:T(8,128)(2,1)S(1)} %get-tuple-element.23.refs_0_), channel_id=1, source_target_pairs={{0,3},{1,2},{2,1},{3,0},{4,7},{5,6},{6,5},{7,4},{8,11},{9,10},{10,... | collective-permute-start | bytes 393224 | tf_op jit(solution)/shard_map/ppermute | solution.py:365
  5.6 16.0 %collective-permute-start.1 = (bf16[16,4096]{1,0:T(8,128)(2,1)S(1)}, bf16[16,4096]{1,0:T(8,128)(2,1)S(1)}, u32[]{:S(2)}, u32[]{:S(2)}) collective-permute-start(bf16[16,4096]{1,0:T(8,128)(2,1)S(1)} %get-tuple-element.23.refs_0_), channel_id=1, source_target_pairs={{0,2},{1,3},{2,0},{3,1},{4,6},{5,7},{6,4},{7,5},{8,10},{9,11},{10,... | collective-permute-start | bytes 393224 | tf_op jit(solution)/shard_map/ppermute | solution.py:365
  5.8 17.1 %collective-permute-start = (bf16[16,4096]{1,0:T(8,128)(2,1)S(1)}, bf16[16,4096]{1,0:T(8,128)(2,1)S(1)}, u32[]{:S(2)}, u32[]{:S(2)}) collective-permute-start(bf16[16,4096]{1,0:T(8,128)(2,1)S(1)} %get-tuple-element.23.refs_0_), channel_id=1, source_target_pairs={{0,1},{1,0},{2,3},{3,2},{4,5},{5,4},{6,7},{7,6},{8,9},{9,8},{10,11... | collective-permute-start | bytes 393224 | tf_op jit(solution)/shard_map/ppermute | solution.py:365
  6.0 7.4 %collective-permute-start.3 = (bf16[16,4096]{1,0:T(8,128)(2,1)S(1)}, bf16[16,4096]{1,0:T(8,128)(2,1)S(1)}, u32[]{:S(2)}, u32[]{:S(2)}) collective-permute-start(bf16[16,4096]{1,0:T(8,128)(2,1)S(1)} %get-tuple-element.24), channel_id=1, source_target_pairs={{0,4},{1,5},{2,6},{3,7},{4,0},{5,1},{6,2},{7,3},{8,12},{9,13},{10,... | collective-permute-start | bytes 393224 | tf_op jit(solution)/shard_map/ppermute | solution.py:365
  8.3 8.2 %collective-permute-start.12 = (bf16[16,4096]{1,0:T(8,128)(2,1)S(1)}, bf16[16,4096]{1,0:T(8,128)(2,1)S(1)}, u32[]{:S(2)}, u32[]{:S(2)}) collective-permute-start(bf16[16,4096]{1,0:T(8,128)(2,1)S(1)} %get-tuple-element.37), channel_id=1, source_target_pairs={{0,4},{1,5},{2,6},{3,7},{4,0},{5,1},{6,2},{7,3},{8,12},{9,13},{10,... | collective-permute-start | bytes 393224 | tf_op jit(solution)/shard_map/ppermute | solution.py:365
  13.4 9.8 %collective-permute-start.6 = (bf16[16,4096]{1,0:T(8,128)(2,1)S(1)}, bf16[16,4096]{1,0:T(8,128)(2,1)S(1)}, u32[]{:S(2)}, u32[]{:S(2)}) collective-permute-start(bf16[16,4096]{1,0:T(8,128)(2,1)S(1)} %collective-permute-done.3.refs_4_), channel_id=1, source_target_pairs={{0,3},{1,2},{2,1},{3,0},{4,7},{5,6},{6,5},{7,4},{8,11},{9,10},{10,... | collective-permute-start | bytes 393224 | tf_op jit(solution)/shard_map/ppermute | solution.py:365
  16.5 7.8 %collective-permute-start.5 = (bf16[16,4096]{1,0:T(8,128)(2,1)S(1)}, bf16[16,4096]{1,0:T(8,128)(2,1)S(1)}, u32[]{:S(2)}, u32[]{:S(2)}) collective-permute-start(bf16[16,4096]{1,0:T(8,128)(2,1)S(1)} %collective-permute-done.3.refs_4_), channel_id=1, source_target_pairs={{0,2},{1,3},{2,0},{3,1},{4,6},{5,7},{6,4},{7,5},{8,10},{9,11},{10,... | collective-permute-start | bytes 393224 | tf_op jit(solution)/shard_map/ppermute | solution.py:365
  19.5 7.0 %collective-permute-start.4 = (bf16[16,4096]{1,0:T(8,128)(2,1)S(1)}, bf16[16,4096]{1,0:T(8,128)(2,1)S(1)}, u32[]{:S(2)}, u32[]{:S(2)}) collective-permute-start(bf16[16,4096]{1,0:T(8,128)(2,1)S(1)} %collective-permute-done.3.refs_4_), channel_id=1, source_target_pairs={{0,1},{1,0},{2,3},{3,2},{4,5},{5,4},{6,7},{7,6},{8,9},{9,8},{10,11... | collective-permute-start | bytes 393224 | tf_op jit(solution)/shard_map/ppermute | solution.py:365
  21.6 28.3 %collective-permute-start.15 = (bf16[32,4096]{1,0:T(8,128)(2,1)S(1)}, bf16[32,4096]{1,0:T(8,128)(2,1)S(1)}, u32[]{:S(2)}, u32[]{:S(2)}) collective-permute-start(bf16[32,4096]{1,0:T(8,128)(2,1)S(1)} %constant_dynamic-update-slice_fusion.refs_0_), channel_id=1, source_target_pairs={{0,3},{1,2},{2,1},{3,0},{4,7},{5,6},{6,5},{7,4},{8,11},{9,10},{10,... | collective-permute-start | bytes 786440 | tf_op jit(solution)/shard_map/ppermute | solution.py:365
  22.8 27.1 %collective-permute-start.14 = (bf16[32,4096]{1,0:T(8,128)(2,1)S(1)}, bf16[32,4096]{1,0:T(8,128)(2,1)S(1)}, u32[]{:S(2)}, u32[]{:S(2)}) collective-permute-start(bf16[32,4096]{1,0:T(8,128)(2,1)S(1)} %constant_dynamic-update-slice_fusion.refs_0_), channel_id=1, source_target_pairs={{0,2},{1,3},{2,0},{3,1},{4,6},{5,7},{6,4},{7,5},{8,10},{9,11},{10,... | collective-permute-start | bytes 786440 | tf_op jit(solution)/shard_map/ppermute | solution.py:365
  23.2 26.7 %collective-permute-start.13 = (bf16[32,4096]{1,0:T(8,128)(2,1)S(1)}, bf16[32,4096]{1,0:T(8,128)(2,1)S(1)}, u32[]{:S(2)}, u32[]{:S(2)}) collective-permute-start(bf16[32,4096]{1,0:T(8,128)(2,1)S(1)} %constant_dynamic-update-slice_fusion.refs_0_), channel_id=1, source_target_pairs={{0,1},{1,0},{2,3},{3,2},{4,5},{5,4},{6,7},{7,6},{8,9},{9,8},{10,11... | collective-permute-start | bytes 786440 | tf_op jit(solution)/shard_map/ppermute | solution.py:365
  41.9 18.8 %collective-permute-start.7 = (bf16[32,4096]{1,0:T(8,128)(2,1)S(1)}, bf16[32,4096]{1,0:T(8,128)(2,1)S(1)}, u32[]{:S(2)}, u32[]{:S(2)}) collective-permute-start(bf16[32,4096]{1,0:T(8,128)(2,1)S(1)} %get-tuple-element.32), channel_id=1, source_target_pairs={{0,1},{1,0},{2,3},{3,2},{4,5},{5,4},{6,7},{7,6},{8,9},{9,8},{10,11... | collective-permute-start | bytes 786440 | tf_op jit(solution)/shard_map/ppermute | solution.py:365
  44.7 16.1 %collective-permute-start.8 = (bf16[32,4096]{1,0:T(8,128)(2,1)S(1)}, bf16[32,4096]{1,0:T(8,128)(2,1)S(1)}, u32[]{:S(2)}, u32[]{:S(2)}) collective-permute-start(bf16[32,4096]{1,0:T(8,128)(2,1)S(1)} %get-tuple-element.33), channel_id=1, source_target_pairs={{0,2},{1,3},{2,0},{3,1},{4,6},{5,7},{6,4},{7,5},{8,10},{9,11},{10,... | collective-permute-start | bytes 786440 | tf_op jit(solution)/shard_map/ppermute | solution.py:365
  49.9 10.9 %collective-permute-start.9 = (bf16[32,4096]{1,0:T(8,128)(2,1)S(1)}, bf16[32,4096]{1,0:T(8,128)(2,1)S(1)}, u32[]{:S(2)}, u32[]{:S(2)}) collective-permute-start(bf16[32,4096]{1,0:T(8,128)(2,1)S(1)} %get-tuple-element.34), channel_id=1, source_target_pairs={{0,3},{1,2},{2,1},{3,0},{4,7},{5,6},{6,5},{7,4},{8,11},{9,10},{10,... | collective-permute-start | bytes 786440 | tf_op jit(solution)/shard_map/ppermute | solution.py:365
  61.0 15.7 %collective-permute-start.11 = (bf16[16,4096]{1,0:T(8,128)(2,1)S(1)}, bf16[16,4096]{1,0:T(8,128)(2,1)S(1)}, u32[]{:S(2)}, u32[]{:S(2)}) collective-permute-start(bf16[16,4096]{1,0:T(8,128)(2,1)S(1)} %get-tuple-element.42), channel_id=1, source_target_pairs={{8,4},{9,5},{10,6},{11,7},{12,0},{13,1},{14,2},{15,3},{16,12},{17,... | collective-permute-start | bytes 393224 | tf_op jit(solution)/shard_map/ppermute | solution.py:373
  68.9 7.7 %collective-permute-start.10 = (bf16[16,4224]{1,0:T(8,128)(2,1)S(1)}, bf16[16,4224]{1,0:T(8,128)(2,1)S(1)}, u32[]{:S(2)}, u32[]{:S(2)}) collective-permute-start(bf16[16,4224]{1,0:T(8,128)(2,1)S(1)} %pad_maximum_fusion), channel_id=1, source_target_pairs={{8,0},{9,1},{10,2},{11,3},{12,4},{13,5},{14,6},{15,7},{16,8},{17,9... | collective-permute-start | bytes 405512 | tf_op jit(solution)/shard_map/ppermute | solution.py:373
